TPU v7x, 256 devices: a whole 4x4x8 slice. The times are simulated.
256 devices in a mesh: segment: 2 (over x_lo), seq: 16 (over y, x_hi, core), mp: 8 (over z).
Axes of the slice: x: 4 (x_hi: 2, x_lo: 2; x = x_hi * 2 + x_lo), y: 4, z: 8, core: 2. Of those that a mesh axis runs over, the one named last changes fastest.
Arguments:
- enc_states: bfloat16 [4096, 4096], P('seq', 'mp'), may hold values from -6 to 6
- dec_states: bfloat16 [4096, 4096], P('seq', 'mp'), may hold values from -21 to 21
- section_weights: bfloat16 [2, 4096, 2, 4096], P('segment', None, None, 'mp'), may hold values from -3 to 3
- group_lengths: int32 [32], P('seq'), may hold values from 1 to 128, 3072 in all
Outputs:
- mixed: bfloat16 [4096, 4096], P('seq', ('segment', 'mp'))
Inputs may be any that keep to these rules, and one draw needn't show every extreme that they name: Rows c * 128 to c * 128 + group_lengths[c] - 1 of the memory are real, the rest of block c is padding.
All inputs are finite; a program needn't handle non-finite values.
Results may differ from a plain program's by a relative error of at most 0.018.
Values may be sent and summed in bfloat16 or wider, within the bound.
A program may use at most 128 MiB of HBM per device.

v0:
```python
import math
import jax
import jax.numpy as jnp
from jax import lax
from jax.sharding import PartitionSpec as P

DH = 256
GROUP = 128


def from_behind(value, axis, steps):
    count = lax.axis_size(axis)
    leading, last = (max(0, -steps), min(count, count - steps))
    return lax.ppermute(value, axis, [(source, source + steps) for source in range(leading, last)])


def local(enc_states, dec_states, section_weights, group_lengths):
    encoder_side = lax.axis_index("segment") == 0
    local_weight = section_weights[0]
    width = local_weight.shape[0]
    columns = local_weight.shape[2]
    enc_rows = enc_states.shape[0]
    dec_rows = dec_states.shape[0]
    heads = columns // DH
    scale = DH ** (-0.5)
    start_sums = (
        jnp.zeros((enc_rows, 2 * columns), jnp.float32),
        jnp.zeros((dec_rows, columns), jnp.float32),
    )
    pieces = (
        lax.all_gather(enc_states, "mp", axis=1, tiled=True),
        lax.all_gather(dec_states, "mp", axis=1, tiled=True),
    )
    rows_in = pieces[0].shape[1]

    def encoder_work(state):
        update = jnp.dot(
            pieces[0],
            local_weight.reshape(rows_in, 2 * columns),
            preferred_element_type=jnp.float32,
        )
        return (update, state[1])

    def decoder_work(state):
        update = jnp.dot(pieces[1], local_weight[:, 0, :], preferred_element_type=jnp.float32)
        return (state[0], update)

    memory_sum, query_sum = lax.cond(encoder_side, encoder_work, decoder_work, start_sums)
    memory = memory_sum.astype(jnp.bfloat16)
    queries = query_sum.astype(jnp.bfloat16).reshape(dec_rows, heads, DH)
    received = from_behind(memory, "segment", 1)
    start_state = (
        jnp.full((dec_rows, heads), -1e30, jnp.float32),
        jnp.zeros((dec_rows, heads), jnp.float32),
        jnp.zeros((dec_rows, heads, DH), jnp.float32),
    )
    carry = start_state
    memory_piece = lax.all_gather(received, "seq", axis=0, tiled=True)
    length_piece = lax.all_gather(group_lengths, "seq", axis=0, tiled=True)
    amount = memory_piece.shape[0]
    span = math.gcd(amount, 1024)
    block_total = amount // span
    memory_blocks = memory_piece.reshape(block_total, span, 2 * columns)
    length_blocks = length_piece.reshape(block_total, span // GROUP)

    def one_block(state, item):
        best, total, accum = state
        block, lengths = item
        block_keys = block[:, :columns].reshape(span, heads, DH)
        block_values = block[:, columns:].reshape(span, heads, DH)
        scores = (
            jnp.einsum("qhd,khd->qhk", queries, block_keys, preferred_element_type=jnp.float32)
            * scale
        )
        valid = (jnp.arange(GROUP)[None, :] < lengths[:, None]).reshape(span)
        scores = jnp.where(valid[None, None, :], scores, -1e30)
        new_best = jnp.maximum(best, jnp.max(scores, axis=2))
        shrink = jnp.exp(best - new_best)
        weights = jnp.exp(scores - new_best[:, :, None]).astype(jnp.bfloat16)
        total = total * shrink + jnp.sum(weights, axis=2, dtype=jnp.float32)
        accum = accum * shrink[:, :, None] + jnp.einsum(
            "qhk,khd->qhd", weights, block_values, preferred_element_type=jnp.float32
        )
        return ((new_best, total, accum), None)

    carry, _ = lax.scan(one_block, carry, (memory_blocks, length_blocks))
    best, total, accum = carry
    attended = (accum / total[:, :, None]).astype(jnp.bfloat16).reshape(dec_rows, columns)

    def no_term(operand):
        return jnp.zeros((dec_rows, width), jnp.float32)

    def output_term(operand):
        projected = lax.dot_general(
            operand,
            local_weight[:, 1, :],
            (((1,), (1,)), ((), ())),
            preferred_element_type=jnp.float32,
        )
        offset = lax.axis_index("mp") * columns
        current = lax.dynamic_slice_in_dim(projected, offset, columns, 1)
        return lax.dynamic_update_slice_in_dim(
            projected, current + dec_states.astype(jnp.float32), offset, 1
        )

    term = lax.cond(encoder_side, no_term, output_term, attended)
    return lax.psum_scatter(
        term.astype(jnp.bfloat16), ("segment", "mp"), scatter_dimension=1, tiled=True
    )


def solution(mesh):
    in_specs = (P("seq", "mp"), P("seq", "mp"), P("segment", None, None, "mp"), P("seq"))
    out_specs = P("seq", ("segment", "mp"))
    return jax.shard_map(local, mesh=mesh, in_specs=in_specs, out_specs=out_specs, check_vma=False)
```

profile of v0, /device:TPU:8, one launch (start us, length us, event | category | flops | bytes accessed | tf_op | source)
XLA Modules:
  0.0 328.2 jit_solution(9274638926449847188)
XLA Ops:
  8.1 8.0 %copy.20 = bf16[1,4096,2,512]{3,1,2,0:T(8,128)(2,1)} copy(bf16[1,4096,2,512]{3,2,1,0:T(2,128)(2,1)} %param.12) | data formatting | bytes 16777216 | tf_op args[2]
  16.0 37.2 %all-gather.6.cloned.1.call-done = bf16[256,4096]{1,0:T(8,128)(2,1)} async-done(((bf16[256,512]{1,0:T(8,128)(2,1)}), bf16[256,4096]{1,0:T(8,128)(2,1)}) %all-gather.6.cloned.1.call-update) | async-done | bytes 2097168 | tf_op jit(solution)/shard_map/all_gather | solution.py:31
  53.2 41.5 %all-gather.4.cloned.1.call-done = bf16[256,4096]{1,0:T(8,128)(2,1)} async-done(((bf16[256,512]{1,0:T(8,128)(2,1)}), bf16[256,4096]{1,0:T(8,128)(2,1)}) %all-gather.4.cloned.1.call-update) | async-done | bytes 2097168 | tf_op jit(solution)/shard_map/all_gather | solution.py:32
  94.7 15.2 %conditional.2 = (bf16[256,1024]{1,0:T(8,128)(2,1)S(1)}, bf16[256,512]{1,0:T(8,128)(2,1)S(1)}) conditional(s32[]{:T(128)} %convert_element_type.25, (bf16[4096,2,512]{2,0,1:T(8,128)(2,1)}, bf16[256,4096]{1,0:T(8,128)(2,1)}) %tuple.67, (bf16[1,4096,2,512]{3,2,1,0:T(2,128)(2,1)}, bf16[256,4096]{1,0:T(8,128)(2,1)}) %tuple.24), branch_computations={%region_0.0_spmd, %region_1.0_spmd} | conditional | flops 2147483648 | bytes 36438064 | solution.py:48
  94.7 9.5 %copy.18 = bf16[512,8,2,512]{3,1,2,0:T(8,128)(2,1)} copy(bf16[512,8,2,512]{3,2,1,0:T(2,128)(2,1)} %bitcast.70) | data formatting | bytes 16777216 | tf_op jit(solution)/shard_map/cond
  104.2 5.7 %fusion.14 = bf16[256,1024]{1,0:T(8,128)(2,1)S(1)} fusion(bf16[256,4096]{1,0:T(8,128)(2,1)S(1)} %copy-done.4, bf16[4096,1024]{1,0:T(8,128)(2,1)} %bitcast.75), kind=kOutput, calls=%fused_computation.28 | convolution fusion | flops 2147483648 | bytes 11010048 | tf_op jit(solution)/shard_map/cond/branch_1_fun/dot_general | solution.py:37
  109.9 1.3 collective-permute-start
  111.2 7.7 %collective-permute-done = bf16[256,1024]{1,0:T(8,128)(2,1)S(1)} collective-permute-done((bf16[256,1024]{1,0:T(8,128)(2,1)S(1)}, bf16[256,1024]{1,0:T(8,128)(2,1)S(1)}, u32[]{:S(2)}, u32[]{:S(2)}) %collective-permute-start) | collective-permute-done | bytes 524320 | tf_op jit(solution)/shard_map/ppermute | solution.py:14
  121.4 12.5 %all-reduce = s32[32]{0:T(128)S(1)} all-reduce(s32[32]{0:T(128)S(1)} %dynamic-update-slice), channel_id=1, replica_groups=mesh['segment'=2,'seq'=16,'mp'=8] {'seq'}, use_global_device_ids=true, to_apply=%add | all-reduce | flops 32 | bytes 256
  134.3 61.9 %all-gather.8.cloned.1.call-done = bf16[4096,1024]{1,0:T(8,128)(2,1)} async-done(((bf16[256,1024]{1,0:T(8,128)(2,1)}), bf16[4096,1024]{1,0:T(8,128)(2,1)}) %all-gather.8.cloned.1.call-update) | async-done | bytes 8388624 | tf_op jit(solution)/shard_map/all_gather | solution.py:58
  196.2 39.4 %while.15 = (s32[]{:T(128)}, f32[256,2]{0,1:T(2,128)S(1)}, f32[256,2]{0,1:T(2,128)S(1)}, f32[256,2,256]{0,2,1:T(8,128)}, s32[4,8]{1,0:T(4,128)S(1)}, /*index=5*/...) while((s32[]{:T(128)}, f32[256,2]{0,1:T(2,128)S(1)}, ...), condition=%wide.region_5.6_spmd.clone, body=%wide.region_2.5_spmd.clone.sunk | while | flops 544083456 | bytes 26513672 | solution.py:86
  196.3 3.1 constant_dynamic-slice_fusion.2
  199.4 2.9 copy.22
  202.5 1.0 bitcast_reduce_fusion.2
  205.3 0.8 copy-done.2
  206.2 3.1 constant_dynamic-slice_fusion.2
  209.3 2.9 copy.22
  212.3 1.0 bitcast_reduce_fusion.2
  215.1 0.8 copy-done.2
  216.0 3.1 constant_dynamic-slice_fusion.2
  219.1 2.9 copy.22
  222.2 1.0 bitcast_reduce_fusion.2
  225.0 0.8 copy-done.2
  225.9 3.1 constant_dynamic-slice_fusion.2
  229.0 2.9 copy.22
  232.0 1.0 bitcast_reduce_fusion.2
  234.8 0.8 copy-done.2
  235.7 1.1 divide_convert_fusion
  236.7 2.5 conditional.3
  236.8 2.5 broadcast.17
  239.2 3.8 %convert_element_type.29 = bf16[256,4096]{1,0:T(8,128)(2,1)} convert(f32[256,4096]{1,0:T(8,128)} %get-tuple-element.217) | non-fusion elementwise | flops 1048576 | bytes 6291456 | tf_op jit(solution)/shard_map/convert_element_type | solution.py:108
  243.1 78.6 %reduce-scatter.2.cloned.1.call-done = bf16[256,256]{1,0:T(8,128)(2,1)} async-done(((bf16[256,4096]{1,0:T(8,128)(2,1)}), bf16[256,256]{1,0:T(8,128)(2,1)}) %reduce-scatter.2.cloned.1.call-update) | async-done | bytes 131088 | tf_op jit(solution)/shard_map/reduce_scatter | solution.py:107
  (70 shorter events, 11.7 us)
Async XLA Ops:
  6.5 46.6 %all-gather.6.cloned.1.call-start = ((), (), s32[]{:S(2)}) async-start(), calls=%async_computation.2 | async-start | bytes 2359296 | tf_op jit(solution)/shard_map/all_gather | solution.py:31
  7.3 87.4 %all-gather.4.cloned.1.call-start = ((), (), s32[]{:S(2)}) async-start(), calls=%async_computation.1 | async-start | bytes 2359296 | tf_op jit(solution)/shard_map/all_gather | solution.py:32
  8.0 188.2 %all-gather.8.cloned.1.call-start = ((), (), s32[]{:S(2)}) async-start(), calls=%async_computation.3 | async-start | bytes 8912896 | tf_op jit(solution)/shard_map/all_gather | solution.py:58
  94.7 25.2 %copy-start.6 = (u32[256]{0:T(256)S(1)}, u32[256]{0:T(256)}, u32[]{:S(2)}) copy-start(u32[256]{0:T(256)} %constant.50) | copy-start | bytes 3076
  94.7 26.5 %copy-start.5 = (s32[2]{0:T(128)S(1)}, s32[2]{0:T(128)}, u32[]{:S(2)}) copy-start(s32[2]{0:T(128)} %param.13) | copy-start | bytes 28
  94.7 9.5 %copy-start.4 = (bf16[256,4096]{1,0:T(8,128)(2,1)S(1)}, bf16[256,4096]{1,0:T(8,128)(2,1)}, u32[]{:S(2)}) copy-start(bf16[256,4096]{1,0:T(8,128)(2,1)} %get-tuple-element.53) | copy-start | bytes 6291460 | tf_op jit(solution)/shard_map/cond
  109.9 9.1 %collective-permute-start = (bf16[256,1024]{1,0:T(8,128)(2,1)S(1)}, bf16[256,1024]{1,0:T(8,128)(2,1)S(1)}, u32[]{:S(2)}, u32[]{:S(2)}) collective-permute-start(bf16[256,1024]{1,0:T(8,128)(2,1)S(1)} %get-tuple-element.70), channel_id=1, source_target_pairs={{0,128},{1,129},{2,130},{3,131},{4,132},{5,133},{6,134},{7,135},{8... | collective-permute-start | bytes 1572872 | tf_op jit(solution)/shard_map/ppermute | solution.py:14
  119.0 0.8 copy-start.3
  119.8 201.9 %reduce-scatter.2.cloned.1.call-start = ((), (), s32[]{:S(2)}) async-start(), calls=%async_computation.4 | async-start | bytes 2228224 | tf_op jit(solution)/shard_map/reduce_scatter | solution.py:107
  203.5 1.0 copy-start.1
  205.3 0.8 copy-start.2
  213.3 1.0 copy-start.1
  215.1 0.8 copy-start.2
  223.2 1.0 copy-start.1
  225.0 0.8 copy-start.2
  233.0 1.0 copy-start.1
  234.8 0.8 copy-start.2
Sparse Core Ops, SparseCore 0:
  9.1 43.9 all-gather.5
  55.0 39.6 all-gather.3
  119.9 76.2 all-gather.7
  243.2 78.4 reduce-scatter.1
where the time goes:
time: 329 us; the launch traced here: 328 us
  waiting for transfers between devices  228 us (69%)
  local copies, waits for them, and re-layouts  51.7 us (16%)
  between operations  13.9 us (4%)
  matrix products  12.7 us (4%)
  blocking collectives  12.5 us (4%)
  other arithmetic  7.33 us (2%)
    reduce_scatter x1, waiting for transfers between devices, local(): lax.psum_scatter(term.astype(jnp.bfloat16), ('segment', 'mp'), scatter_di...  78.6 us
    all_gather x1, waiting for transfers between devices, local(): memory_piece = lax.all_gather(received, 'seq', axis=0, tiled=True)  61.9 us
    all_gather x1, waiting for transfers between devices, local(): lax.all_gather(dec_states, 'mp', axis=1, tiled=True)  41.5 us
    all_gather x1, waiting for transfers between devices, local(): lax.all_gather(enc_states, 'mp', axis=1, tiled=True)  37.2 us
    dynamic_slice x8, local copies, waits for them, and re-layouts, local(): carry, _ = lax.scan(one_block, carry, (memory_blocks, length_blocks))  23.8 us
    unnamed x1, blocking collectives  12.5 us
    unnamed x11, local copies, waits for them, and re-layouts  9.78 us
    cond x3, local copies, waits for them, and re-layouts  9.49 us
  transfers between devices with their start and end apart: 5, of which 5 were waited for; matrix products, arithmetic and copies ran while one was open for 3% of the time, Pallas kernels for 0%

commit v1 on v0

--- a/solution.py
+++ b/solution.py
@@ -6,6 +6,19 @@
 
 DH = 256
 GROUP = 128
+
+
+def ring_gather(x, axis, dim):
+    ways = lax.axis_size(axis)
+    up = [(d, (d + 1) % ways) for d in range(ways)]
+    down = [(d, (d - 1) % ways) for d in range(ways)]
+    earlier, later = ([x], [x])
+    for _ in range(ways // 2):
+        earlier.append(lax.ppermute(earlier[-1], axis, up))
+    for _ in range((ways - 1) // 2):
+        later.append(lax.ppermute(later[-1], axis, down))
+    line = jnp.concatenate([*earlier[::-1], *later[1:]], axis=dim)
+    return jnp.roll(line, (lax.axis_index(axis) - ways // 2) * x.shape[dim], axis=dim)
 
 
 def from_behind(value, axis, steps):
@@ -29,7 +42,7 @@
     )
     pieces = (
         lax.all_gather(enc_states, "mp", axis=1, tiled=True),
-        lax.all_gather(dec_states, "mp", axis=1, tiled=True),
+        ring_gather(dec_states, "mp", 1),
     )
     rows_in = pieces[0].shape[1]
 

time: 329 us -> 302 us (0.918)
  waiting for transfers between devices: 228 us -> 186 us
  starting transfers between devices: 1.44 us -> 13.5 us
  matrix products: 12.7 us -> 18.9 us
    all_gather x1 -> x0, waiting for transfers between devices: 41.5 us -> none  [local(): lax.all_gather(dec_states, 'mp', axis=1, tiled=True)]
    all_gather x1, waiting for transfers between devices: 37.2 us -> 0.01 us  [local(): lax.all_gather(enc_states, 'mp', axis=1, tiled=True)]
    ppermute x0 -> x7, waiting for transfers between devices: none -> 33.5 us  [the longest x4 30.1 us: ring_gather(): earlier.append(lax.ppermute(earlier[-1], axis, up))]
    ppermute x0 -> x7, starting transfers between devices: none -> 12 us  [the longest x3 10 us: ring_gather(): later.append(lax.ppermute(later[-1], axis, down))]
    dot_general x4, matrix products: 2.95 us -> 9.14 us  [one_block(): jnp.einsum('qhk,khd->qhd', weights, block_values, preferred_element_type=...]
    while x20 -> x4, local copies, waits for them, and re-layouts: 5.21 us -> 0.01 us
    all_gather x1, waiting for transfers between devices: 61.9 us -> 65.5 us  [local(): memory_piece = lax.all_gather(received, 'seq', axis=0, tiled=True)]
    unnamed x11 -> x30, local copies, waits for them, and re-layouts: 9.78 us -> 12.2 us
  transfers between devices with their start and end apart: 5 -> 11, of which waited for: 5 -> 9; matrix products, arithmetic and copies ran while one was open for 3% -> 3% of each run, Pallas kernels for 0% -> 0%
where the time goes in v1:
time: 302 us; the launch traced here: 301 us
  waiting for transfers between devices  186 us (62%)
  local copies, waits for them, and re-layouts  48.9 us (16%)
  matrix products  18.9 us (6%)
  between operations  14 us (5%)
  starting transfers between devices  13.5 us (4%)
  blocking collectives  12.4 us (4%)
  other arithmetic  7.32 us (2%)
    reduce_scatter x1, waiting for transfers between devices, local(): lax.psum_scatter(term.astype(jnp.bfloat16), ('segment', 'mp'), scatter_di...  78.6 us
    all_gather x1, waiting for transfers between devices, local(): memory_piece = lax.all_gather(received, 'seq', axis=0, tiled=True)  65.5 us
    ppermute x4, waiting for transfers between devices, ring_gather(): earlier.append(lax.ppermute(earlier[-1], axis, up))  30.1 us
    dynamic_slice x8, local copies, waits for them, and re-layouts, local(): carry, _ = lax.scan(one_block, carry, (memory_blocks, length_blocks))  23.8 us
    unnamed x1, blocking collectives  12.4 us
    unnamed x30, local copies, waits for them, and re-layouts  12.2 us
    ppermute x3, starting transfers between devices, ring_gather(): later.append(lax.ppermute(later[-1], axis, down))  10 us
    cond x3, local copies, waits for them, and re-layouts  9.47 us
  transfers between devices with their start and end apart: 11, of which 9 were waited for; matrix products, arithmetic and copies ran while one was open for 3% of the time, Pallas kernels for 0%

profile of v1, /device:TPU:8, one launch (start us, length us, event | category | flops | bytes accessed | tf_op | source)
XLA Modules:
  0.0 301.3 jit_solution(9978434688633188064)
XLA Ops:
  7.3 2.0 collective-permute-start
  9.3 10.5 %collective-permute-done = bf16[256,512]{1,0:T(8,128)(2,1)S(1)} collective-permute-done((bf16[256,512]{1,0:T(8,128)(2,1)}, bf16[256,512]{1,0:T(8,128)(2,1)S(1)}, u32[]{:S(2)}, u32[]{:S(2)}) %collective-permute-start) | collective-permute-done | bytes 262176 | tf_op jit(solution)/shard_map/ppermute | solution.py:17
  19.8 3.2 %collective-permute-start.4 = (bf16[256,512]{1,0:T(8,128)(2,1)}, bf16[256,512]{1,0:T(8,128)(2,1)S(1)}, u32[]{:S(2)}, u32[]{:S(2)}) collective-permute-start(bf16[256,512]{1,0:T(8,128)(2,1)} %param.11), channel_id=1, source_target_pairs={{0,7},{1,0},{2,1},{3,2},{4,3},{5,4},{6,5},{7,6},{8,15},{9,8},{10,9... | collective-permute-start | bytes 786440 | tf_op jit(solution)/shard_map/ppermute | solution.py:19
  23.0 8.6 %collective-permute-done.1 = bf16[256,512]{1,0:T(8,128)(2,1)S(1)} collective-permute-done((bf16[256,512]{1,0:T(8,128)(2,1)S(1)}, bf16[256,512]{1,0:T(8,128)(2,1)S(1)}, u32[]{:S(2)}, u32[]{:S(2)}) %collective-permute-start.1) | collective-permute-done | bytes 262176 | tf_op jit(solution)/shard_map/ppermute | solution.py:17
  33.4 3.6 %collective-permute-start.5 = (bf16[256,512]{1,0:T(8,128)(2,1)S(1)}, bf16[256,512]{1,0:T(8,128)(2,1)S(1)}, u32[]{:S(2)}, u32[]{:S(2)}) collective-permute-start(bf16[256,512]{1,0:T(8,128)(2,1)S(1)} %collective-permute-done.4), channel_id=1, source_target_pairs={{0,7},{1,0},{2,1},{3,2},{4,3},{5,4},{6,5},{7,6},{8,15},{9,8},{10,9... | collective-permute-start | bytes 786440 | tf_op jit(solution)/shard_map/ppermute | solution.py:19
  37.0 9.0 %collective-permute-done.2 = bf16[256,512]{1,0:T(8,128)(2,1)S(1)} collective-permute-done((bf16[256,512]{1,0:T(8,128)(2,1)S(1)}, bf16[256,512]{1,0:T(8,128)(2,1)S(1)}, u32[]{:S(2)}, u32[]{:S(2)}) %collective-permute-start.2) | collective-permute-done | bytes 262176 | tf_op jit(solution)/shard_map/ppermute | solution.py:17
  46.0 8.1 %copy.20 = bf16[1,4096,2,512]{3,1,2,0:T(8,128)(2,1)} copy(bf16[1,4096,2,512]{3,2,1,0:T(2,128)(2,1)} %param.12) | data formatting | bytes 16777216 | tf_op args[2]
  54.0 3.2 %collective-permute-start.6 = (bf16[256,512]{1,0:T(8,128)(2,1)S(1)}, bf16[256,512]{1,0:T(8,128)(2,1)S(1)}, u32[]{:S(2)}, u32[]{:S(2)}) collective-permute-start(bf16[256,512]{1,0:T(8,128)(2,1)S(1)} %collective-permute-done.5), channel_id=1, source_target_pairs={{0,7},{1,0},{2,1},{3,2},{4,3},{5,4},{6,5},{7,6},{8,15},{9,8},{10,9... | collective-permute-start | bytes 786440 | tf_op jit(solution)/shard_map/ppermute | solution.py:19
  57.3 2.1 collective-permute-done.3
  61.5 1.9 copy-done.3
  63.4 15.2 %conditional.2 = (bf16[256,1024]{1,0:T(8,128)(2,1)S(1)}, bf16[256,512]{1,0:T(8,128)(2,1)S(1)}) conditional(s32[]{:T(128)} %convert_element_type.25, (s32[]{:T(128)}, s32[]{:T(128)}, bf16[256,8192]{1,0:T(8,128)(2,1)}, bf16[4096,2,512]{2,0,1:T(8,128)(2,1)}, s32[]{:T(128)}, /*index=5*/s32[]{:T(128)}) %tuple.83, ...), branch_computations={%region_0.1_spmd.clone, %region_1.2_spmd} | conditional | flops 2147483648 | bytes 36438064 | solution.py:61
  63.4 9.5 %copy.18 = bf16[512,8,2,512]{3,1,2,0:T(8,128)(2,1)} copy(bf16[512,8,2,512]{3,2,1,0:T(2,128)(2,1)} %bitcast.69) | data formatting | bytes 16777216 | tf_op jit(solution)/shard_map/cond
  72.9 5.7 %fusion.16 = bf16[256,1024]{1,0:T(8,128)(2,1)S(1)} fusion(bf16[256,4096]{1,0:T(8,128)(2,1)S(1)} %copy-done.4, bf16[4096,1024]{1,0:T(8,128)(2,1)} %bitcast.74), kind=kOutput, calls=%fused_computation.46 | convolution fusion | flops 2147483648 | bytes 11010048 | tf_op jit(solution)/shard_map/cond/branch_1_fun/dot_general | solution.py:50
  79.9 7.9 %collective-permute-done.7 = bf16[256,1024]{1,0:T(8,128)(2,1)S(1)} collective-permute-done((bf16[256,1024]{1,0:T(8,128)(2,1)S(1)}, bf16[256,1024]{1,0:T(8,128)(2,1)S(1)}, u32[]{:S(2)}, u32[]{:S(2)}) %collective-permute-start.7) | collective-permute-done | bytes 524320 | tf_op jit(solution)/shard_map/ppermute | solution.py:27
  90.3 12.4 %all-reduce = s32[32]{0:T(128)S(1)} all-reduce(s32[32]{0:T(128)S(1)} %dynamic-update-slice), channel_id=1, replica_groups=mesh['segment'=2,'seq'=16,'mp'=8] {'seq'}, use_global_device_ids=true, to_apply=%add | all-reduce | flops 32 | bytes 256
  103.1 65.5 %all-gather.5.cloned.1.call-done = bf16[4096,1024]{1,0:T(8,128)(2,1)} async-done(((bf16[256,1024]{1,0:T(8,128)(2,1)}), bf16[4096,1024]{1,0:T(8,128)(2,1)}) %all-gather.5.cloned.1.call-update) | async-done | bytes 8388624 | tf_op jit(solution)/shard_map/all_gather | solution.py:71
  168.6 40.3 %while.15 = (s32[]{:T(128)}, f32[256,2]{0,1:T(2,128)S(1)}, f32[256,2]{0,1:T(2,128)S(1)}, f32[256,2,256]{0,2,1:T(8,128)}, s32[4,8]{1,0:T(4,128)S(1)}, /*index=5*/...) while((s32[]{:T(128)}, f32[256,2]{0,1:T(2,128)S(1)}, ...), condition=%wide.region_5.6_spmd.clone, body=%wide.region_2.5_spmd.clone.sunk | while | flops 544083456 | bytes 22319312 | solution.py:99
  168.6 3.1 %constant_dynamic-slice_fusion.2 = bf16[1,1024,1024]{2,1,0:T(8,128)(2,1)} fusion(bf16[4,1024,1024]{2,1,0:T(8,128)(2,1)} %get-tuple-element.308, s32[]{:T(128)} %get-tuple-element.294), kind=kLoop, calls=%fused_computation.26.clone.1 | loop fusion | bytes 4194308 | tf_op jit(solution)/shard_map/while/body/jit(dynamic_index_in_dim)/dynamic_slice | solution.py:99
  171.7 2.9 copy.22
  177.9 3.1 %constant_dynamic-slice_fusion.2 = bf16[1,1024,1024]{2,1,0:T(8,128)(2,1)} fusion(bf16[4,1024,1024]{2,1,0:T(8,128)(2,1)} %get-tuple-element.308, s32[]{:T(128)} %get-tuple-element.294), kind=kLoop, calls=%fused_computation.26.clone.1 | loop fusion | bytes 4194308 | tf_op jit(solution)/shard_map/while/body/jit(dynamic_index_in_dim)/dynamic_slice | solution.py:99
  181.0 2.9 copy.22
  185.6 2.5 fusion.40
  188.2 3.1 %constant_dynamic-slice_fusion.2 = bf16[1,1024,1024]{2,1,0:T(8,128)(2,1)} fusion(bf16[4,1024,1024]{2,1,0:T(8,128)(2,1)} %get-tuple-element.308, s32[]{:T(128)} %get-tuple-element.294), kind=kLoop, calls=%fused_computation.26.clone.1 | loop fusion | bytes 4194308 | tf_op jit(solution)/shard_map/while/body/jit(dynamic_index_in_dim)/dynamic_slice | solution.py:99
  191.3 2.9 copy.22
  195.9 2.5 fusion.40
  198.6 3.1 %constant_dynamic-slice_fusion.2 = bf16[1,1024,1024]{2,1,0:T(8,128)(2,1)} fusion(bf16[4,1024,1024]{2,1,0:T(8,128)(2,1)} %get-tuple-element.308, s32[]{:T(128)} %get-tuple-element.294), kind=kLoop, calls=%fused_computation.26.clone.1 | loop fusion | bytes 4194308 | tf_op jit(solution)/shard_map/while/body/jit(dynamic_index_in_dim)/dynamic_slice | solution.py:99
  201.7 2.9 copy.22
  206.3 2.5 fusion.40
  209.9 2.5 conditional.3
  209.9 2.5 broadcast.18
  212.4 3.8 %convert_element_type.29 = bf16[256,4096]{1,0:T(8,128)(2,1)} convert(f32[256,4096]{1,0:T(8,128)} %get-tuple-element.312) | non-fusion elementwise | flops 1048576 | bytes 6291456 | tf_op jit(solution)/shard_map/convert_element_type | solution.py:121
  216.2 78.6 %reduce-scatter.2.cloned.1.call-done = bf16[256,256]{1,0:T(8,128)(2,1)} async-done(((bf16[256,4096]{1,0:T(8,128)(2,1)}), bf16[256,256]{1,0:T(8,128)(2,1)}) %reduce-scatter.2.cloned.1.call-update) | async-done | bytes 131088 | tf_op jit(solution)/shard_map/reduce_scatter | solution.py:120
  (85 shorter events, 17.7 us)
Async XLA Ops:
  6.5 56.9 %all-gather.3.cloned.1.call-start = ((), (), s32[]{:S(2)}) async-start(), calls=%async_computation.1 | async-start | bytes 2359296 | tf_op jit(solution)/shard_map/all_gather | solution.py:44
  7.3 161.3 %all-gather.5.cloned.1.call-start = ((), (), s32[]{:S(2)}) async-start(), calls=%async_computation.2 | async-start | bytes 8912896 | tf_op jit(solution)/shard_map/all_gather | solution.py:71
  7.3 12.5 %collective-permute-start = (bf16[256,512]{1,0:T(8,128)(2,1)}, bf16[256,512]{1,0:T(8,128)(2,1)S(1)}, u32[]{:S(2)}, u32[]{:S(2)}) collective-permute-start(bf16[256,512]{1,0:T(8,128)(2,1)} %param.11), channel_id=1, source_target_pairs={{0,1},{1,2},{2,3},{3,4},{4,5},{5,6},{6,7},{7,0},{8,9},{9,10},{10,1... | collective-permute-start | bytes 786440 | tf_op jit(solution)/shard_map/ppermute | solution.py:17
  19.8 11.9 %collective-permute-start.1 = (bf16[256,512]{1,0:T(8,128)(2,1)S(1)}, bf16[256,512]{1,0:T(8,128)(2,1)S(1)}, u32[]{:S(2)}, u32[]{:S(2)}) collective-permute-start(bf16[256,512]{1,0:T(8,128)(2,1)S(1)} %collective-permute-done), channel_id=1, source_target_pairs={{0,1},{1,2},{2,3},{3,4},{4,5},{5,6},{6,7},{7,0},{8,9},{9,10},{10,1... | collective-permute-start | bytes 786440 | tf_op jit(solution)/shard_map/ppermute | solution.py:17
  19.8 13.7 %collective-permute-start.4 = (bf16[256,512]{1,0:T(8,128)(2,1)}, bf16[256,512]{1,0:T(8,128)(2,1)S(1)}, u32[]{:S(2)}, u32[]{:S(2)}) collective-permute-start(bf16[256,512]{1,0:T(8,128)(2,1)} %param.11), channel_id=1, source_target_pairs={{0,7},{1,0},{2,1},{3,2},{4,3},{5,4},{6,5},{7,6},{8,15},{9,8},{10,9... | collective-permute-start | bytes 786440 | tf_op jit(solution)/shard_map/ppermute | solution.py:19
  31.6 14.3 %collective-permute-start.2 = (bf16[256,512]{1,0:T(8,128)(2,1)S(1)}, bf16[256,512]{1,0:T(8,128)(2,1)S(1)}, u32[]{:S(2)}, u32[]{:S(2)}) collective-permute-start(bf16[256,512]{1,0:T(8,128)(2,1)S(1)} %collective-permute-done.1), channel_id=1, source_target_pairs={{0,1},{1,2},{2,3},{3,4},{4,5},{5,6},{6,7},{7,0},{8,9},{9,10},{10,1... | collective-permute-start | bytes 786440 | tf_op jit(solution)/shard_map/ppermute | solution.py:17
  33.4 20.6 %collective-permute-start.5 = (bf16[256,512]{1,0:T(8,128)(2,1)S(1)}, bf16[256,512]{1,0:T(8,128)(2,1)S(1)}, u32[]{:S(2)}, u32[]{:S(2)}) collective-permute-start(bf16[256,512]{1,0:T(8,128)(2,1)S(1)} %collective-permute-done.4), channel_id=1, source_target_pairs={{0,7},{1,0},{2,1},{3,2},{4,3},{5,4},{6,5},{7,6},{8,15},{9,8},{10,9... | collective-permute-start | bytes 786440 | tf_op jit(solution)/shard_map/ppermute | solution.py:19
  46.0 13.4 %collective-permute-start.3 = (bf16[256,512]{1,0:T(8,128)(2,1)S(1)}, bf16[256,512]{1,0:T(8,128)(2,1)S(1)}, u32[]{:S(2)}, u32[]{:S(2)}) collective-permute-start(bf16[256,512]{1,0:T(8,128)(2,1)S(1)} %collective-permute-done.2), channel_id=1, source_target_pairs={{0,1},{1,2},{2,3},{3,4},{4,5},{5,6},{6,7},{7,0},{8,9},{9,10},{10,1... | collective-permute-start | bytes 786440 | tf_op jit(solution)/shard_map/ppermute | solution.py:17
  46.0 13.5 %copy-start = (bf16[256,512]{1,0:T(8,128)(2,1)S(1)}, bf16[256,512]{1,0:T(8,128)(2,1)}, u32[]{:S(2)}) copy-start(bf16[256,512]{1,0:T(8,128)(2,1)} %param.11) | copy-start | bytes 786436
  54.0 7.1 %collective-permute-start.6 = (bf16[256,512]{1,0:T(8,128)(2,1)S(1)}, bf16[256,512]{1,0:T(8,128)(2,1)S(1)}, u32[]{:S(2)}, u32[]{:S(2)}) collective-permute-start(bf16[256,512]{1,0:T(8,128)(2,1)S(1)} %collective-permute-done.5), channel_id=1, source_target_pairs={{0,7},{1,0},{2,1},{3,2},{4,3},{5,4},{6,5},{7,6},{8,15},{9,8},{10,9... | collective-permute-start | bytes 786440 | tf_op jit(solution)/shard_map/ppermute | solution.py:19
  61.4 1.9 copy-start.3
  63.4 25.3 %copy-start.6 = (u32[256]{0:T(256)S(1)}, u32[256]{0:T(256)}, u32[]{:S(2)}) copy-start(u32[256]{0:T(256)} %constant.94) | copy-start | bytes 3076
  63.4 26.7 %copy-start.5 = (s32[2]{0:T(128)S(1)}, s32[2]{0:T(128)}, u32[]{:S(2)}) copy-start(s32[2]{0:T(128)} %param.13) | copy-start | bytes 28
  63.4 9.5 %copy-start.4 = (bf16[256,4096]{1,0:T(8,128)(2,1)S(1)}, bf16[256,4096]{1,0:T(8,128)(2,1)}, u32[]{:S(2)}) copy-start(bf16[256,4096]{1,0:T(8,128)(2,1)} %get-tuple-element.128) | copy-start | bytes 6291460 | tf_op jit(solution)/shard_map/cond
  78.6 9.2 %collective-permute-start.7 = (bf16[256,1024]{1,0:T(8,128)(2,1)S(1)}, bf16[256,1024]{1,0:T(8,128)(2,1)S(1)}, u32[]{:S(2)}, u32[]{:S(2)}) collective-permute-start(bf16[256,1024]{1,0:T(8,128)(2,1)S(1)} %get-tuple-element.145), channel_id=1, source_target_pairs={{0,128},{1,129},{2,130},{3,131},{4,132},{5,133},{6,134},{7,135},{8... | collective-permute-start | bytes 1572872 | tf_op jit(solution)/shard_map/ppermute | solution.py:27
  87.8 0.8 copy-start.2
  88.6 206.2 %reduce-scatter.2.cloned.1.call-start = ((), (), s32[]{:S(2)}) async-start(), calls=%async_computation.3 | async-start | bytes 2228224 | tf_op jit(solution)/shard_map/reduce_scatter | solution.py:120
Sparse Core Ops, SparseCore 0:
  9.1 50.7 all-gather.2
  88.8 79.7 all-gather.4
  216.3 78.4 reduce-scatter.1
